TPU v7x, 512 devices: a whole 4x4x16 slice. The times are simulated.
512 devices in a mesh: dp: 64 (over y, z), mp: 8 (over x, core).
Axes of the slice: x: 4, y: 4, z: 16, core: 2. Of those that a mesh axis runs over, the one named last changes fastest.
Arguments:
- x_in: bfloat16 [25600, 2048], P('dp'), may hold values from -6 to 6
- cotangent: bfloat16 [25600, 7168], P('dp', 'mp'), may hold values from -6 to 6
- w_gate: bfloat16 [2048, 7168], P('dp', 'mp'), may hold values from -0.125 to 0.125
- w_up: bfloat16 [2048, 7168], P('dp', 'mp'), may hold values from -0.125 to 0.125
- send_counts: int32 [64, 64], P('dp'), may hold values from 0 to 4, as said below
- recv_counts: int32 [64, 64], P('dp'), may hold values from 0 to 4, as said below
Outputs:
- grad_x: bfloat16 [25600, 2048], P('dp', 'mp')
- grad_gate: float32 [2048, 7168], P('dp', 'mp')
Inputs may be any that keep to these rules, and one draw needn't show every extreme that they name: `send_counts`: each entry is 0 to 4. A quarter of the indices only send and the rest only receive; one sending index sends 4 rows to every receiver, so its live rows reach 400. recv_counts is the transpose of send_counts.
All inputs are finite; a program needn't handle non-finite values.
Results may differ from a plain program's by a relative error of at most 0.014.
Values may be sent and summed in bfloat16 or wider, within the bound.
A program may use at most 64 MiB of HBM per device.

v0:
```python
import jax
import jax.numpy as jnp
from jax import lax
from jax.sharding import PartitionSpec as P

BAL = 208


def contract_last(left, right):
    return lax.dot_general(
        left, right, (((1,), (1,)), ((), ())), preferred_element_type=jnp.float32
    )


def swiglu_back(x_rows, cot_rows, gate_full, up_full, live_mask):
    gate_val = jnp.dot(x_rows, gate_full, preferred_element_type=jnp.float32)
    up_val = jnp.dot(x_rows, up_full, preferred_element_type=jnp.float32)
    sig = jax.nn.sigmoid(gate_val)
    cot_val = cot_rows.astype(jnp.float32)
    d_gate = jnp.where(
        live_mask[:, None], cot_val * up_val * sig * (1.0 + gate_val * (1.0 - sig)), 0.0
    ).astype(jnp.bfloat16)
    d_up = jnp.where(live_mask[:, None], cot_val * gate_val * sig, 0.0).astype(jnp.bfloat16)
    partial_value = contract_last(d_gate, gate_full) + contract_last(d_up, up_full)
    return (partial_value, d_gate)


def group_sum(partial_value):
    return lax.psum_scatter(
        partial_value.astype(jnp.bfloat16), "mp", scatter_dimension=1, tiled=True
    )


def on_device(x_in, cotangent, w_gate, w_up, send_counts, recv_counts):
    rows_cap = x_in.shape[0]
    width = x_in.shape[1]
    dev_count = lax.axis_size("dp")
    gate_full, up_full = (
        lax.all_gather(w_gate, "dp", axis=0, tiled=True),
        lax.all_gather(w_up, "dp", axis=0, tiled=True),
    )
    sent = send_counts[0]
    got = recv_counts[0]
    live_rows = BAL + jnp.sum(sent) - jnp.sum(got)
    live_mask = jnp.arange(rows_cap) < live_rows
    partial_value, d_gate = swiglu_back(x_in, cotangent, gate_full, up_full, live_mask)
    grad_x = group_sum(partial_value)
    block_rows = width // dev_count
    whole = lax.dot_general(
        x_in, d_gate, (((0,), (0,)), ((), ())), preferred_element_type=jnp.float32
    )
    grad_gate = lax.psum_scatter(
        whole.astype(jnp.bfloat16), "dp", scatter_dimension=0, tiled=True
    ).astype(jnp.float32)
    return (grad_x, grad_gate)


def solution(mesh):
    return jax.shard_map(
        on_device,
        mesh=mesh,
        in_specs=(
            P("dp", None),
            P("dp", "mp"),
            P("dp", "mp"),
            P("dp", "mp"),
            P("dp", None),
            P("dp", None),
        ),
        out_specs=(P("dp", "mp"), P("dp", "mp")),
        check_vma=False,
    )
```

profile of v0, /device:TPU:8, one launch (start us, length us, event | category | flops | bytes accessed | tf_op | source)
XLA Modules:
  0.0 1060.5 jit_solution(8219626550588682840)
XLA Ops:
  7.2 0.0 copy-start
  7.2 0.0 all-gather.5.cloned.1.call-start
  7.2 0.7 all-gather.5.cloned.1.call-update
  7.9 0.0 all-gather.3.cloned.1.call-start
  8.0 0.7 all-gather.3.cloned.1.call-update
  8.7 0.0 reduce-scatter.7.cloned.1.call-start
  8.7 1.3 reduce_sum.19
  10.0 1.3 reduce_sum.18
  12.6 0.0 copy-start.2
  12.6 147.1 %all-gather.5.cloned.1.call-done = bf16[2048,896]{1,0:T(8,128)(2,1)} async-done(((bf16[32,896]{1,0:T(8,128)(2,1)}), bf16[2048,896]{1,0:T(8,128)(2,1)}) %all-gather.5.cloned.1.call-update) | async-done | bytes 3670032 | tf_op jit(solution)/shard_map/all_gather | solution.py:39
  159.7 0.0 copy-done
  159.7 5.0 fusion.11
  164.7 137.7 %all-gather.3.cloned.1.call-done = bf16[2048,896]{1,0:T(8,128)(2,1)} async-done(((bf16[32,896]{1,0:T(8,128)(2,1)}), bf16[2048,896]{1,0:T(8,128)(2,1)}) %all-gather.3.cloned.1.call-update) | async-done | bytes 3670032 | tf_op jit(solution)/shard_map/all_gather | solution.py:40
  302.4 0.0 copy-done.2
  302.4 4.6 select_convert_fusion
  307.0 4.0 convert_bitcast_fusion
  311.0 6.1 copy.10
  317.1 0.0 reduce-scatter.7.cloned.1.call-update
  317.2 0.0 reduce-scatter.5.cloned.1.call-start
  317.2 0.0 copy-start.1
  317.2 0.0 copy-start.3
  317.2 4.1 fusion.12
  321.3 0.0 copy-done.1
  321.3 0.0 copy-done.3
  321.3 3.1 add_convert_fusion
  324.5 0.0 reduce-scatter.5.cloned.1.call-update
  324.5 687.3 %reduce-scatter.7.cloned.1.call-done = bf16[32,896]{1,0:T(8,128)(2,1)} async-done(((bf16[2048,896]{1,0:T(8,128)(2,1)}), bf16[32,896]{1,0:T(8,128)(2,1)}) %reduce-scatter.7.cloned.1.call-update) | async-done | bytes 57360
  1011.7 1.0 copy.11
  1012.7 0.8 copy.9
  1013.5 40.4 %reduce-scatter.5.cloned.1.call-done = bf16[400,256]{1,0:T(8,128)(2,1)} async-done(((bf16[400,2048]{1,0:T(8,128)(2,1)}), bf16[400,256]{1,0:T(8,128)(2,1)}) %reduce-scatter.5.cloned.1.call-update) | async-done | bytes 204816 | tf_op jit(solution)/shard_map/reduce_scatter | solution.py:29
  (1 shorter events, 0.0 us)
Async XLA Ops:
  7.2 152.6 %copy-start = (bf16[400,2048]{1,0:T(8,128)(2,1)S(1)}, bf16[400,2048]{1,0:T(8,128)(2,1)}, u32[]{:S(2)}) copy-start(bf16[400,2048]{1,0:T(8,128)(2,1)} %param.6) | copy-start | bytes 4915204
  7.2 152.5 %all-gather.5.cloned.1.call-start = ((), (), s32[]{:S(2)}) async-start(), calls=%async_computation.3 | async-start | bytes 3727360 | tf_op jit(solution)/shard_map/all_gather | solution.py:39
  7.9 294.5 %all-gather.3.cloned.1.call-start = ((), (), s32[]{:S(2)}) async-start(), calls=%async_computation.2 | async-start | bytes 3727360 | tf_op jit(solution)/shard_map/all_gather | solution.py:40
  8.7 1003.1 %reduce-scatter.7.cloned.1.call-start = ((), (), s32[]{:S(2)}) async-start(), calls=%async_computation.5 | async-start | bytes 3727360
  12.6 289.8 %copy-start.2 = (bf16[400,896]{1,0:T(8,128)(2,1)S(1)}, bf16[400,896]{1,0:T(8,128)(2,1)}, u32[]{:S(2)}) copy-start(bf16[400,896]{1,0:T(8,128)(2,1)} %param.7) | copy-start | bytes 2150404
  317.2 736.8 %reduce-scatter.5.cloned.1.call-start = ((), (), s32[]{:S(2)}) async-start(), calls=%async_computation.4 | async-start | bytes 1843200 | tf_op jit(solution)/shard_map/reduce_scatter | solution.py:29
  317.2 4.1 copy-start.1
  317.2 4.1 copy-start.3
Sparse Core Ops, SparseCore 0:
  11.0 148.7 all-gather.4
  162.7 139.7 all-gather.2
  317.3 694.4 reduce-scatter.6
  1015.3 38.6 reduce-scatter.4
where the time goes:
time: 1060 us
  waiting for transfers between devices  1010 us (95%)
  matrix products  20.8 us (2%)
  between operations  15.1 us (1%)
    unnamed x5, waiting for transfers between devices  689 us
    all_gather x1, waiting for transfers between devices, on_device(): lax.all_gather(w_gate, 'dp', axis=0, tiled=True)  147 us
    all_gather x1, waiting for transfers between devices, on_device(): lax.all_gather(w_up, 'dp', axis=0, tiled=True)  138 us
    reduce_scatter x1, waiting for transfers between devices, group_sum(): lax.psum_scatter(partial_value.astype(jnp.bfloat16), 'mp', scatter_dimens...  40.4 us
  transfers between devices with their start and end apart: 4, of which 4 were waited for; matrix products, arithmetic and copies ran while one was open for 2% of the time, Pallas kernels for 0%

commit v1 on v0

--- a/solution.py
+++ b/solution.py
@@ -2,6 +2,7 @@
 import jax.numpy as jnp
 from jax import lax
 from jax.sharding import PartitionSpec as P
+from jax.lax import all_to_all, axis_size
 
 BAL = 208
 
@@ -37,7 +38,7 @@
     dev_count = lax.axis_size("dp")
     gate_full, up_full = (
         lax.all_gather(w_gate, "dp", axis=0, tiled=True),
-        lax.all_gather(w_up, "dp", axis=0, tiled=True),
+        jnp.concatenate(all_to_all(jnp.stack(axis_size("dp") * [w_up]), "dp", 0, 0), axis=0),
     )
     sent = send_counts[0]
     got = recv_counts[0]

time: 1060 us -> 995 us (0.939)
  waiting for transfers between devices: 1010 us -> 925 us
  starting transfers between devices: 0.16 us -> 19.2 us
    all_gather x1 -> x0, waiting for transfers between devices: 138 us -> none  [on_device(): lax.all_gather(w_up, 'dp', axis=0, tiled=True)]
    all_gather x1, waiting for transfers between devices: 147 us -> 198 us  [on_device(): lax.all_gather(w_gate, 'dp', axis=0, tiled=True)]
    all_to_all x0 -> x1, starting transfers between devices: none -> 19 us  [on_device(): all_to_all(jnp.stack(axis_size('dp') * [w_up]), 'dp', 0, 0)]
    unnamed x5 -> x4, waiting for transfers between devices: 689 us -> 687 us
  transfers between devices with their start and end apart: 4 -> 4, of which waited for: 4 -> 3; matrix products, arithmetic and copies ran while one was open for 2% -> 2% of each run, Pallas kernels for 0% -> 0%
where the time goes in v1:
time: 995 us; the launch traced here: 994 us
  waiting for transfers between devices  925 us (93%)
  matrix products  22.8 us (2%)
  starting transfers between devices  19.2 us (2%)
  between operations  15.1 us (2%)
  local copies, waits for them, and re-layouts  11 us (1%)
    unnamed x4, waiting for transfers between devices  687 us
    all_gather x1, waiting for transfers between devices, on_device(): lax.all_gather(w_gate, 'dp', axis=0, tiled=True)  198 us
    reduce_scatter x1, waiting for transfers between devices, group_sum(): lax.psum_scatter(partial_value.astype(jnp.bfloat16), 'mp', scatter_dimens...  40.5 us
  transfers between devices with their start and end apart: 4, of which 3 were waited for; matrix products, arithmetic and copies ran while one was open for 2% of the time, Pallas kernels for 0%

profile of v1, /device:TPU:8, one launch (start us, length us, event | category | flops | bytes accessed | tf_op | source)
XLA Modules:
  0.0 994.3 jit_solution(2987062269486212313)
XLA Ops:
  7.2 0.0 copy-start
  7.2 3.1 stack.2
  10.3 0.0 copy-start.2
  10.3 0.0 copy-start.3
  10.3 19.0 %all-to-all-start = ((bf16[64,32,896]{2,1,0:T(8,128)(2,1)}), bf16[64,32,896]{2,1,0:T(8,128)(2,1)}, u32[]{:S(2)}, u32[]{:S(2)}) async-start(bf16[64,32,896]{2,1,0:T(8,128)(2,1)} %stack.2), calls=%async_computation | async-start | bytes 7340032 | tf_op jit(solution)/shard_map/all_to_all | solution.py:41
  29.3 0.0 all-gather.2.cloned.1.call-start
  29.4 0.7 all-gather.2.cloned.1.call-update
  30.1 0.0 reduce-scatter.7.cloned.1.call-start
  30.1 0.0 copy-done.2
  30.1 0.6 reduce_sum.19
  30.8 0.0 copy-done.3
  30.8 0.6 reduce_sum.18
  32.7 0.0 copy-start.1
  32.7 197.7 %all-gather.2.cloned.1.call-done = bf16[2048,896]{1,0:T(8,128)(2,1)} async-done(((bf16[32,896]{1,0:T(8,128)(2,1)}), bf16[2048,896]{1,0:T(8,128)(2,1)}) %all-gather.2.cloned.1.call-update) | async-done | bytes 3670032 | tf_op jit(solution)/shard_map/all_gather | solution.py:40
  230.5 0.0 copy-done
  230.5 5.0 fusion.11
  235.5 0.0 all-to-all-done
  235.5 0.0 copy-done.1
  235.5 4.6 select_convert_fusion
  240.1 4.0 convert_bitcast_fusion
  244.1 6.1 copy.10
  250.2 0.0 reduce-scatter.7.cloned.1.call-update
  250.2 0.0 reduce-scatter.5.cloned.1.call-start
  250.3 0.0 copy-start.4
  250.3 4.0 fusion.12
  254.3 0.0 copy-done.4
  254.3 5.2 add_convert_fusion
  259.6 0.0 reduce-scatter.5.cloned.1.call-update
  259.6 685.8 %reduce-scatter.7.cloned.1.call-done = bf16[32,896]{1,0:T(8,128)(2,1)} async-done(((bf16[2048,896]{1,0:T(8,128)(2,1)}), bf16[32,896]{1,0:T(8,128)(2,1)}) %reduce-scatter.7.cloned.1.call-update) | async-done | bytes 57360
  945.4 1.0 copy.11
  946.4 0.8 copy.9
  947.2 40.5 %reduce-scatter.5.cloned.1.call-done = bf16[400,256]{1,0:T(8,128)(2,1)} async-done(((bf16[400,2048]{1,0:T(8,128)(2,1)}), bf16[400,256]{1,0:T(8,128)(2,1)}) %reduce-scatter.5.cloned.1.call-update) | async-done | bytes 204816 | tf_op jit(solution)/shard_map/reduce_scatter | solution.py:30
  (1 shorter events, 0.0 us)
Async XLA Ops:
  7.2 223.3 %copy-start = (bf16[400,2048]{1,0:T(8,128)(2,1)S(1)}, bf16[400,2048]{1,0:T(8,128)(2,1)}, u32[]{:S(2)}) copy-start(bf16[400,2048]{1,0:T(8,128)(2,1)} %param.6) | copy-start | bytes 4915204
  10.3 19.8 %copy-start.2 = (s32[1,64]{1,0:T(1,128)S(1)}, s32[1,64]{1,0:T(1,128)}, u32[]{:S(2)}) copy-start(s32[1,64]{1,0:T(1,128)} %param.11) | copy-start | bytes 772
  10.3 20.5 %copy-start.3 = (s32[1,64]{1,0:T(1,128)S(1)}, s32[1,64]{1,0:T(1,128)}, u32[]{:S(2)}) copy-start(s32[1,64]{1,0:T(1,128)} %param.10) | copy-start | bytes 772
  10.3 225.2 %all-to-all-start = ((bf16[64,32,896]{2,1,0:T(8,128)(2,1)}), bf16[64,32,896]{2,1,0:T(8,128)(2,1)}, u32[]{:S(2)}, u32[]{:S(2)}) async-start(bf16[64,32,896]{2,1,0:T(8,128)(2,1)} %stack.2), calls=%async_computation | async-start | bytes 7340032 | tf_op jit(solution)/shard_map/all_to_all | solution.py:41
  29.3 201.1 %all-gather.2.cloned.1.call-start = ((), (), s32[]{:S(2)}) async-start(), calls=%async_computation.3 | async-start | bytes 3727360 | tf_op jit(solution)/shard_map/all_gather | solution.py:40
  30.1 915.3 %reduce-scatter.7.cloned.1.call-start = ((), (), s32[]{:S(2)}) async-start(), calls=%async_computation.5 | async-start | bytes 3727360
  32.7 202.8 %copy-start.1 = (bf16[400,896]{1,0:T(8,128)(2,1)S(1)}, bf16[400,896]{1,0:T(8,128)(2,1)}, u32[]{:S(2)}) copy-start(bf16[400,896]{1,0:T(8,128)(2,1)} %param.7) | copy-start | bytes 2150404
  250.2 737.5 %reduce-scatter.5.cloned.1.call-start = ((), (), s32[]{:S(2)}) async-start(), calls=%async_computation.4 | async-start | bytes 1843200 | tf_op jit(solution)/shard_map/reduce_scatter | solution.py:30
  250.3 4.0 copy-start.4
Sparse Core Ops, SparseCore 0:
  33.1 197.2 all-gather.1
  250.4 695.0 reduce-scatter.6
  949.1 38.5 reduce-scatter.4
